TPU v7x, 32 devices: a whole 2x2x4 slice. The times are simulated.
32 devices in a mesh: dp: 8 (over z, y), tensor: 4 (over x, core).
Axes of the slice: x: 2, y: 2, z: 4, core: 2. Of those that a mesh axis runs over, the one named last changes fastest.
Arguments:
- query_act: bfloat16 [8, 1024, 1024], P('dp', None, 'tensor'), may hold values from -6 to 6
- rotated_keys: bfloat16 [8, 1024, 256], P('dp'), may hold values from -6 to 6
- value_input: bfloat16 [8, 1024, 256], P('dp'), may hold values from -6 to 6
- grad_out: bfloat16 [8, 1024, 8192], P('dp', 'tensor'), may hold values from -6 to 6
- out_weight: bfloat16 [1024, 8192], P('tensor', 'dp'), may hold values from -0.1875 to 0.1875
- doc_lengths: int32 [8, 4], P('dp'), may hold values from 1 to 512, 1024 in all within a row
Outputs:
- query_grad: bfloat16 [8, 1024, 1024], P('dp', None, 'tensor')
- key_gradient: bfloat16 [8, 4, 512, 128], P('dp', 'tensor')
- value_gradient: bfloat16 [8, 4, 512, 128], P('dp', 'tensor')
- weight_grad: float32 [1024, 8192], P('tensor', 'dp')
All inputs are finite; a program needn't handle non-finite values.
Results may differ from a plain program's by a relative error of at most 0.015.
The roundings to bfloat16 on the way count: a program that leaves them out, or rounds other values in their place, can miss the bound.
Values may be sent and summed in bfloat16 or wider, within the bound.
A program may use at most 128 MiB of HBM per device.

v0:
```python
import jax
import jax.numpy as jnp
from jax import lax
from jax.sharding import PartitionSpec as P

HEAD_SIZE = 128


def swapped(value, axis, apart):
    mask = 2**apart
    pairs = [(source, source ^ mask) for source in range(lax.axis_size(axis))]
    return lax.ppermute(value, axis, pairs)


def shards(query_act, rotated_keys, value_input, grad_out, out_weight, doc_lengths):
    score_scale = HEAD_SIZE ** (-0.5)
    tensor_index = lax.axis_index("tensor")
    kv_group = tensor_index // 2
    own_half = tensor_index % 2
    seq_len = query_act.shape[1]
    head_count = query_act.shape[2] // HEAD_SIZE
    query_heads = query_act[0].reshape(seq_len, head_count, HEAD_SIZE).transpose(1, 0, 2)
    key_rows = lax.dynamic_slice_in_dim(rotated_keys[0], kv_group * HEAD_SIZE, HEAD_SIZE, 1)
    value_rows = lax.dynamic_slice_in_dim(value_input[0], kv_group * HEAD_SIZE, HEAD_SIZE, 1)
    doc_ends = jnp.cumsum(doc_lengths[0])
    positions = jnp.arange(seq_len, dtype=jnp.int32)
    doc_ids = jnp.sum((positions[:, None] >= doc_ends[None, :]).astype(jnp.int32), axis=1)
    block_rows = min(512, seq_len)
    block_count = seq_len // block_rows
    full_weight = lax.all_gather(out_weight, "dp", axis=1, tiled=True)

    def key_reach():
        return seq_len

    def masked_scores(block_idx, key_span):
        first = block_idx * block_rows
        query_block = query_heads[:, first : first + block_rows]
        scores = (
            jnp.einsum("hqd,kd->hqk", query_block, key_rows, preferred_element_type=jnp.float32)
            * score_scale
        )
        allowed = (positions[None, :key_span] <= positions[first : first + block_rows, None]) & (
            doc_ids[None, :key_span] == doc_ids[first : first + block_rows, None]
        )
        return jnp.where(allowed[None], scores, -jnp.inf)

    totals_list = []
    outputs_list = []
    for block_idx in range(block_count):
        key_span = key_reach()
        scores = masked_scores(block_idx, key_span)
        row_max = jnp.max(scores, axis=-1, keepdims=True)
        log_total = row_max + jnp.log(jnp.sum(jnp.exp(scores - row_max), axis=-1, keepdims=True))
        prob_bf16 = jnp.exp(scores - log_total).astype(jnp.bfloat16)
        outputs_list.append(
            jnp.einsum(
                "hqk,kd->hqd", prob_bf16, value_rows, preferred_element_type=jnp.float32
            ).astype(jnp.bfloat16)
        )
        totals_list.append(log_total)
    attn_out = jnp.concatenate(outputs_list, axis=1)
    out_flat = attn_out.transpose(1, 0, 2).reshape(seq_len, head_count * HEAD_SIZE)
    local_rows = grad_out[0]
    gathered = lax.all_gather(local_rows, "tensor", axis=0, tiled=True)
    out_grad = jnp.einsum(
        "sd,hd->sh", gathered, full_weight, preferred_element_type=jnp.float32
    ).astype(jnp.bfloat16)
    weight_part = jnp.einsum("sh,sd->hd", out_flat, gathered, preferred_element_type=jnp.float32)
    weight_grad = lax.psum_scatter(weight_part, "dp", scatter_dimension=1, tiled=True)
    grad_heads = out_grad.reshape(seq_len, head_count, HEAD_SIZE).transpose(1, 0, 2)
    key_accum = jnp.zeros((seq_len, HEAD_SIZE), jnp.float32)
    value_accum = jnp.zeros((seq_len, HEAD_SIZE), jnp.float32)
    query_list = []
    for block_idx in range(block_count):
        key_span = key_reach()
        first = block_idx * block_rows
        scores = masked_scores(block_idx, key_span)
        prob_block = jnp.exp(scores - totals_list[block_idx])
        prob_bf16 = prob_block.astype(jnp.bfloat16)
        grad_block = grad_heads[:, first : first + block_rows]
        out_block = attn_out[:, first : first + block_rows]
        query_block = query_heads[:, first : first + block_rows]
        dprobs = jnp.einsum(
            "hqd,kd->hqk", grad_block, value_rows, preferred_element_type=jnp.float32
        )
        row_delta = jnp.sum(
            grad_block.astype(jnp.float32) * out_block.astype(jnp.float32), axis=-1, keepdims=True
        )
        score_gradient = (prob_block * (dprobs - row_delta) * score_scale).astype(jnp.bfloat16)
        query_list.append(
            jnp.einsum(
                "hqk,kd->hqd", score_gradient, key_rows, preferred_element_type=jnp.float32
            ).astype(jnp.bfloat16)
        )
        key_accum = key_accum.at[:key_span].add(
            jnp.einsum(
                "hqk,hqd->kd", score_gradient, query_block, preferred_element_type=jnp.float32
            )
        )
        value_accum = value_accum.at[:key_span].add(
            jnp.einsum("hqk,hqd->kd", prob_bf16, grad_block, preferred_element_type=jnp.float32)
        )
    query_grad = (
        jnp.concatenate(query_list, axis=1)
        .transpose(1, 0, 2)
        .reshape(1, seq_len, head_count * HEAD_SIZE)
    )
    half_rows = seq_len // 2
    other_start = (1 - own_half) * half_rows
    outgoing = (
        lax.dynamic_slice_in_dim(key_accum, other_start, half_rows, 0),
        lax.dynamic_slice_in_dim(value_accum, other_start, half_rows, 0),
    )
    partner = swapped((outgoing[0], outgoing[1]), "tensor", 0)
    key_mine = lax.dynamic_slice_in_dim(key_accum, own_half * half_rows, half_rows, 0) + partner[0]
    value_mine = (
        lax.dynamic_slice_in_dim(value_accum, own_half * half_rows, half_rows, 0) + partner[1]
    )
    key_gradient = key_mine.astype(jnp.bfloat16).reshape(1, 1, half_rows, HEAD_SIZE)
    value_gradient = value_mine.astype(jnp.bfloat16).reshape(1, 1, half_rows, HEAD_SIZE)
    return (query_grad, key_gradient, value_gradient, weight_grad)


def solution(mesh):
    placed = (
        P("dp", None, "tensor"),
        P("dp", None, None),
        P("dp", None, None),
        P("dp", "tensor", None),
        P("tensor", "dp"),
        P("dp", None),
    )
    return jax.shard_map(
        shards,
        mesh=mesh,
        in_specs=placed,
        out_specs=(
            P("dp", None, "tensor"),
            P("dp", "tensor", None, None),
            P("dp", "tensor", None, None),
            P("tensor", "dp"),
        ),
        check_vma=False,
    )
```

profile of v0, /device:TPU:0, one launch (start us, length us, event | category | flops | bytes accessed | tf_op | source)
XLA Modules:
  0.0 374.6 jit_solution(8681585686457070649)
XLA Ops:
  7.2 0.0 copy-start
  7.2 0.0 copy-start.10
  7.2 0.0 copy-start.5
  7.2 0.0 copy-start.8
  7.2 0.0 all-gather.4.cloned.1.call-start
  7.3 0.7 all-gather.4.cloned.1.call-update
  7.9 0.0 all-gather.6.cloned.1.call-start
  8.0 0.7 all-gather.6.cloned.1.call-update
  8.7 0.0 reduce-scatter.2.cloned.1.call-start
  8.8 0.0 copy-done.10
  8.8 0.2 reduce-window.8
  9.0 0.0 copy-done.5
  9.0 0.2 copy.29
  9.2 0.3 copy.30
  9.5 0.1 convert_reduce_fusion
  9.6 0.9 fusion.9
  10.5 0.0 copy-done.8
  10.5 0.9 fusion.7
  11.4 0.0 copy-start.1
  11.4 0.9 fusion.6
  12.4 0.0 copy-start.3
  12.4 2.2 exponential_reduce_fusion
  14.5 0.1 copy-done.3
  14.7 0.0 copy-done.1
  14.7 0.0 copy-done
  14.7 1.6 convolution_convert_fusion.1
  16.2 69.5 %all-gather.4.cloned.1.call-done = bf16[256,8192]{1,0:T(8,128)(2,1)} async-done(((bf16[256,1024]{1,0:T(8,128)(2,1)}), bf16[256,8192]{1,0:T(8,128)(2,1)}) %all-gather.4.cloned.1.call-update) | async-done | bytes 4194320 | tf_op jit(solution)/shard_map/all_gather | solution.py:30
  85.7 106.0 %all-gather.6.cloned.1.call-done = bf16[1,1024,8192]{2,1,0:T(8,128)(2,1)} async-done(((bf16[1,256,8192]{2,1,0:T(8,128)(2,1)}), bf16[1,1024,8192]{2,1,0:T(8,128)(2,1)}) %all-gather.6.cloned.1.call-update) | async-done | bytes 16777232 | tf_op jit(solution)/shard_map/all_gather | solution.py:64
  191.8 11.5 %fusion.10 = bf16[1024,256]{0,1:T(8,128)(2,1)S(1)} fusion(bf16[256,8192]{1,0:T(8,128)(2,1)} %all-gather.4.cloned.1.call-done, bf16[1,1024,8192]{2,1,0:T(8,128)(2,1)} %all-gather.6.cloned.1.call-done), kind=kOutput, calls=%fused_computation.20 | convolution fusion | flops 4295229440 | bytes 21495808 | tf_op jit(solution)/shard_map/sd,hd->sh/dot_general | solution.py:65
  203.2 0.3 copy.31
  203.5 0.0 copy-start.6
  203.5 3.8 %multiply_reduce_fusion.1 = (f32[2,512]{1,0:T(2,128)S(1)}, f32[2,512]{1,0:T(2,128)S(1)}, bf16[2,512,128]{2,1,0:T(8,128)(2,1)S(1)}) fusion(bf16[2,1024,128]{2,1,0:T(8,128)(2,1)S(1)} %bitcast.100, bf16[2,512,128]{2,1,0:T(8,128)(2,1)S(1)} %convolution_convert_fusion.1, bf16[1,1024,256]{2,1,0:T(8,128)(2,1)S(1)} %copy-done, s32[]{:T(128)S(6)} %select_n.33, ...), kind=kOutput, calls=%fused_computation.34 | convolution fusion | flops 273807360 | bytes 6041604 | tf_op jit(solution)/shard_map/hqk,kd->hqd/dot_general | solution.py:56
  207.3 0.0 copy-done.6
  207.4 0.2 copy.39
  207.6 12.5 %fusion = f32[256,8192]{1,0:T(8,128)} fusion(bf16[1024,256]{0,1:T(8,128)(2,1)S(1)} %bitcast.93, bf16[1,1024,8192]{2,1,0:T(8,128)(2,1)} %all-gather.6.cloned.1.call-done), kind=kOutput, calls=%fused_computation | convolution fusion | flops 4294967296 | bytes 25690112 | tf_op jit(solution)/shard_map/sh,sd->hd/dot_general | solution.py:68
  220.1 0.0 copy-start.7
  220.1 0.0 reduce-scatter.2.cloned.1.call-update
  220.1 1.0 copy-done.7
  221.1 0.0 copy-start.4
  221.1 4.0 %multiply_convert_fusion = bf16[2,512,1024]{1,2,0:T(8,128)(2,1)S(1)} fusion(f32[1024,2,512]{2,0,1:T(8,128)} %copy-done.1, f32[2,512]{1,0:T(2,128)S(1)} %get-tuple-element.93, f32[2,512]{1,0:T(2,128)S(1)} %log_add_fusion, pred[512,1024]{0,1:T(8,128)(4,1)S(1)} %get-tuple-element.94, bf16[2,1024,128]{2,1,0:T(8,128)(2,1)S(1)} %bitcast.101, ...), kind=kOutput, calls=%fused_computation.6 | convolution fusion | flops 275775488 | bytes 7348228 | tf_op jit(solution)/shard_map/hqd,kd->hqk/dot_general | solution.py:83
  225.1 0.7 convolution_bitcast_fusion.2
  225.8 0.0 copy-done.4
  225.8 0.0 copy-start.9
  225.8 1.7 multiply_convert_fusion.1
  227.5 0.0 copy-start.2
  227.5 0.7 fusion.13
  228.3 0.3 collective-permute-start
  228.6 0.0 copy-done.9
  228.6 0.8 convolution_convert_fusion
  229.4 0.4 copy-done.2
  229.8 1.1 convolution_bitcast_fusion
  230.8 1.3 fusion.14
  232.1 0.8 convolution_convert_fusion.2
  232.9 0.3 collective-permute-start.1
  233.3 0.2 copy.38
  233.5 1.0 copy.40
  234.5 0.0 collective-permute-done
  234.5 0.7 fusion.41
  235.2 0.0 collective-permute-done.1
  235.2 1.6 fusion.42
  236.8 131.3 %reduce-scatter.2.cloned.1.call-done = f32[256,1024]{1,0:T(8,128)} async-done(((f32[256,8192]{1,0:T(8,128)}), f32[256,1024]{1,0:T(8,128)}) %reduce-scatter.2.cloned.1.call-update) | async-done | bytes 1048592 | tf_op jit(solution)/shard_map/reduce_scatter | solution.py:69
  (11 shorter events, 0.2 us)
Async XLA Ops:
  7.2 7.5 %copy-start = (bf16[1,1024,256]{2,1,0:T(8,128)(2,1)S(1)}, bf16[1,1024,256]{2,1,0:T(8,128)(2,1)}, u32[]{:S(2)}) copy-start(bf16[1,1024,256]{2,1,0:T(8,128)(2,1)} %param.24) | copy-start | bytes 1572868
  7.2 1.6 copy-start.10
  7.2 1.8 copy-start.5
  7.2 3.3 copy-start.8
  7.2 78.5 %all-gather.4.cloned.1.call-start = ((), (), s32[]{:S(2)}) async-start(), calls=%async_computation.1 | async-start | bytes 4718592 | tf_op jit(solution)/shard_map/all_gather | solution.py:30
  7.9 183.8 %all-gather.6.cloned.1.call-start = ((), (), s32[]{:S(2)}) async-start(), calls=%async_computation.3 | async-start | bytes 20971520 | tf_op jit(solution)/shard_map/all_gather | solution.py:64
  8.7 359.4 %reduce-scatter.2.cloned.1.call-start = ((), (), s32[]{:S(2)}) async-start(), calls=%async_computation.2 | async-start | bytes 9437184 | tf_op jit(solution)/shard_map/reduce_scatter | solution.py:69
  11.4 3.2 copy-start.1
  12.4 2.3 copy-start.3
  203.5 3.8 %copy-start.6 = (bf16[1024,2,128]{2,0,1:T(8,128)(2,1)}, bf16[1024,2,128]{2,0,1:T(8,128)(2,1)S(1)}, u32[]{:S(2)}) copy-start(bf16[1024,2,128]{2,0,1:T(8,128)(2,1)S(1)} %copy.31) | copy-start | bytes 1572868
  220.1 1.0 copy-start.7
  221.1 4.7 %copy-start.4 = (f32[1024,2,512]{2,0,1:T(8,128)S(1)}, f32[1024,2,512]{2,0,1:T(8,128)}, u32[]{:S(2)}) copy-start(f32[1024,2,512]{2,0,1:T(8,128)} %copy-done.3) | copy-start | bytes 12582916
  225.8 2.8 copy-start.9
  227.5 2.3 copy-start.2
  228.3 6.2 %collective-permute-start = (f32[512,128]{1,0:T(8,128)S(1)}, f32[512,128]{1,0:T(8,128)S(1)}, u32[]{:S(2)}, u32[]{:S(2)}) collective-permute-start(f32[512,128]{1,0:T(8,128)S(1)} %constant_dynamic-slice_fusion.1), channel_id=1, source_target_pairs={{0,1},{1,0},{2,3},{3,2},{4,5},{5,4},{6,7},{7,6},{8,9},{9,8},{10,11... | collective-permute-start | bytes 786440 | tf_op jit(solution)/shard_map/ppermute | solution.py:12
  232.9 2.3 collective-permute-start.1
Sparse Core Ops, SparseCore 0:
  10.2 75.4 all-gather.3
  87.3 104.4 all-gather.5
  220.2 147.8 reduce-scatter.1
where the time goes:
time: 375 us
  waiting for transfers between devices  308 us (82%)
  matrix products  42.1 us (11%)
  between operations  14.1 us (4%)
  other arithmetic  5.72 us (2%)
  local copies, waits for them, and re-layouts  3.8 us (1%)
    reduce_scatter x1, waiting for transfers between devices, shards(): lax.psum_scatter(weight_part, 'dp', scatter_dimension=1, tiled=True)  131 us
    all_gather x1, waiting for transfers between devices, shards(): gathered = lax.all_gather(local_rows, 'tensor', axis=0, tiled=True)  106 us
    all_gather x1, waiting for transfers between devices, shards(): full_weight = lax.all_gather(out_weight, 'dp', axis=1, tiled=True)  69.5 us
    dot_general x1, matrix products, shards(): jnp.einsum('sh,sd->hd', out_flat, gathered, preferred_element_type=jnp.fl...  12.5 us
    dot_general x1, matrix products, shards(): jnp.einsum('sd,hd->sh', gathered, full_weight, preferred_element_type=jnp...  11.5 us
  transfers between devices with their start and end apart: 5, of which 3 were waited for; matrix products, arithmetic and copies ran while one was open for 6% of the time, Pallas kernels for 0%

commit v1 on v0

--- a/solution.py
+++ b/solution.py
@@ -27,7 +27,12 @@
     doc_ids = jnp.sum((positions[:, None] >= doc_ends[None, :]).astype(jnp.int32), axis=1)
     block_rows = min(512, seq_len)
     block_count = seq_len // block_rows
-    full_weight = lax.all_gather(out_weight, "dp", axis=1, tiled=True)
+    ring = [out_weight]
+    for hop in range(7):
+        ring.append(lax.ppermute(ring[-1], "dp", [(dev, (dev + 1) % 8) for dev in range(8)]))
+    full_weight = jnp.roll(
+        jnp.concatenate(ring[::-1], axis=1), (lax.axis_index("dp") + 1) * ring[0].shape[1], axis=1
+    )
 
     def key_reach():
         return seq_len

time: 375 us -> 310 us (0.83)
  waiting for transfers between devices: 308 us -> 214 us
  local copies, waits for them, and re-layouts: 3.8 us -> 24.5 us
  matrix products: 42.1 us -> 46.9 us
    all_gather x1, waiting for transfers between devices: 106 us -> 0.01 us  [shards(): gathered = lax.all_gather(local_rows, 'tensor', axis=0, tiled=True)]
    ppermute x0 -> x7, waiting for transfers between devices: none -> 86.5 us  [shards(): lax.ppermute(ring[-1], 'dp', [(dev, (dev + 1) % 8) for dev in range(8)])]
    all_gather x1 -> x0, waiting for transfers between devices: 69.5 us -> none  [shards(): full_weight = lax.all_gather(out_weight, 'dp', axis=1, tiled=True)]
    unnamed x24 -> x57, local copies, waits for them, and re-layouts: 2.76 us -> 21.9 us
    reduce_scatter x1, waiting for transfers between devices: 131 us -> 127 us  [shards(): lax.psum_scatter(weight_part, 'dp', scatter_dimension=1, tiled=True)]
  transfers between devices with their start and end apart: 5 -> 11, of which waited for: 3 -> 8; matrix products, arithmetic and copies ran while one was open for 6% -> 15% of each run, Pallas kernels for 0% -> 0%
where the time goes in v1:
time: 310 us; the launch traced here: 309 us
  waiting for transfers between devices  214 us (69%)
  matrix products  46.9 us (15%)
  local copies, waits for them, and re-layouts  24.5 us (8%)
  between operations  14.5 us (5%)
  other arithmetic  5.53 us (2%)
  starting transfers between devices  3.23 us (1%)
    reduce_scatter x1, waiting for transfers between devices, shards(): lax.psum_scatter(weight_part, 'dp', scatter_dimension=1, tiled=True)  127 us
    ppermute x7, waiting for transfers between devices, shards(): lax.ppermute(ring[-1], 'dp', [(dev, (dev + 1) % 8) for dev in range(8)])  86.5 us
    unnamed x57, local copies, waits for them, and re-layouts  21.9 us
    dot_general x1, matrix products, shards(): jnp.einsum('sh,sd->hd', out_flat, gathered, preferred_element_type=jnp.fl...  12.7 us
    dot_general x1, matrix products, shards(): jnp.einsum('sd,hd->sh', gathered, full_weight, preferred_element_type=jnp...  11.6 us
    dot_general x2, matrix products, shards(): jnp.einsum('hqk,kd->hqd', prob_bf16, value_rows, preferred_element_type=j...  7.6 us
  transfers between devices with their start and end apart: 11, of which 8 were waited for; matrix products, arithmetic and copies ran while one was open for 15% of the time, Pallas kernels for 0%

profile of v1, /device:TPU:0, one launch (start us, length us, event | category | flops | bytes accessed | tf_op | source)
XLA Modules:
  0.0 309.0 jit_solution(2205856693941327589)
XLA Ops:
  7.2 0.0 copy-start
  7.2 0.0 all-gather.3.cloned.1.call-start
  7.3 0.7 all-gather.3.cloned.1.call-update
  7.9 0.0 reduce-scatter.2.cloned.1.call-start
  8.0 0.3 copy-done.5
  8.3 3.0 collective-permute-start
  11.3 15.0 %collective-permute-done = bf16[256,1024]{1,0:T(8,128)(2,1)S(1)} collective-permute-done((bf16[256,1024]{1,0:T(8,128)(2,1)S(1)}, bf16[256,1024]{1,0:T(8,128)(2,1)S(1)}, u32[]{:S(2)}, u32[]{:S(2)}) %collective-permute-start) | collective-permute-done | bytes 524320 | tf_op jit(solution)/shard_map/ppermute | solution.py:32
  26.2 15.8 %collective-permute-done.1 = bf16[256,1024]{1,0:T(8,128)(2,1)S(1)} collective-permute-done((bf16[256,1024]{1,0:T(8,128)(2,1)S(1)}, bf16[256,1024]{1,0:T(8,128)(2,1)S(1)}, u32[]{:S(2)}, u32[]{:S(2)}) %collective-permute-start.1) | collective-permute-done | bytes 524320 | tf_op jit(solution)/shard_map/ppermute | solution.py:32
  42.0 0.2 reduce-window.8
  42.2 0.2 copy.29
  42.4 1.0 copy.30
  43.4 0.1 convert_reduce_fusion
  43.5 13.5 %collective-permute-done.2 = bf16[256,1024]{1,0:T(8,128)(2,1)} collective-permute-done((bf16[256,1024]{1,0:T(8,128)(2,1)S(1)}, bf16[256,1024]{1,0:T(8,128)(2,1)}, u32[]{:S(2)}, u32[]{:S(2)}) %collective-permute-start.2) | collective-permute-done | bytes 524320 | tf_op jit(solution)/shard_map/ppermute | solution.py:32
  57.1 0.9 fusion.10
  58.0 13.4 %collective-permute-done.3 = bf16[256,1024]{1,0:T(8,128)(2,1)S(1)} collective-permute-done((bf16[256,1024]{1,0:T(8,128)(2,1)}, bf16[256,1024]{1,0:T(8,128)(2,1)S(1)}, u32[]{:S(2)}, u32[]{:S(2)}) %collective-permute-start.3) | collective-permute-done | bytes 524320 | tf_op jit(solution)/shard_map/ppermute | solution.py:32
  71.3 2.1 fusion.7
  73.5 0.9 fusion.8
  74.5 10.1 %collective-permute-done.4 = bf16[256,1024]{1,0:T(8,128)(2,1)S(1)} collective-permute-done((bf16[256,1024]{1,0:T(8,128)(2,1)S(1)}, bf16[256,1024]{1,0:T(8,128)(2,1)S(1)}, u32[]{:S(2)}, u32[]{:S(2)}) %collective-permute-start.4) | collective-permute-done | bytes 524320 | tf_op jit(solution)/shard_map/ppermute | solution.py:32
  84.6 2.0 exponential_reduce_fusion
  86.6 10.4 %collective-permute-done.5 = bf16[256,1024]{1,0:T(8,128)(2,1)} collective-permute-done((bf16[256,1024]{1,0:T(8,128)(2,1)S(1)}, bf16[256,1024]{1,0:T(8,128)(2,1)}, u32[]{:S(2)}, u32[]{:S(2)}) %collective-permute-start.5) | collective-permute-done | bytes 524320 | tf_op jit(solution)/shard_map/ppermute | solution.py:32
  97.0 0.0 collective-permute-start.6
  97.1 0.0 copy-start.9
  97.1 3.8 %convolution_convert_fusion.1 = bf16[2,512,128]{2,1,0:T(8,128)(2,1)S(1)} fusion(bf16[1,1024,256]{2,1,0:T(8,128)(2,1)S(1)} %copy-done, s32[]{:T(128)S(6)} %select_n.45, f32[1024,2,512]{2,0,1:T(8,128)} %copy-done.3, f32[2,512]{1,0:T(2,128)S(1)} %log_add_fusion, pred[512,1024]{0,1:T(8,128)(4,1)S(1)} %get-tuple-element.94), kind=kOutput, calls=%fused_computation.29 | convolution fusion | flops 272760832 | bytes 5246980 | tf_op jit(solution)/shard_map/hqk,kd->hqd/dot_general | solution.py:61
  100.9 8.3 %collective-permute-done.6 = bf16[256,1024]{1,0:T(8,128)(2,1)} collective-permute-done((bf16[256,1024]{1,0:T(8,128)(2,1)}, bf16[256,1024]{1,0:T(8,128)(2,1)}, u32[]{:S(2)}, u32[]{:S(2)}) %collective-permute-start.6) | collective-permute-done | bytes 524320 | tf_op jit(solution)/shard_map/ppermute | solution.py:32
  109.2 1.9 constant_dynamic-update-slice_fusion.15
  111.1 1.9 constant_dynamic-update-slice_fusion.14
  113.0 0.9 constant_dynamic-update-slice_fusion.13
  113.9 0.9 constant_dynamic-update-slice_fusion.12
  114.8 1.9 constant_dynamic-update-slice_fusion.11
  116.7 0.8 constant_dynamic-update-slice_fusion.10
  117.5 0.8 constant_dynamic-update-slice_fusion.9
  118.3 0.9 constant_dynamic-update-slice_fusion.8
  119.2 1.9 constant_dynamic-update-slice_fusion.7
  121.1 1.9 constant_dynamic-update-slice_fusion.6
  123.0 0.8 constant_dynamic-update-slice_fusion.5
  123.9 0.8 constant_dynamic-update-slice_fusion.4
  124.7 1.9 constant_dynamic-update-slice_fusion.3
  126.6 0.8 constant_dynamic-update-slice_fusion.2
  127.4 0.8 constant_dynamic-update-slice_fusion.1
  128.2 0.9 constant_dynamic-update-slice_fusion
  129.1 11.6 %fusion.11 = bf16[256,1024]{1,0:T(8,128)(2,1)S(1)} fusion(bf16[1,1024,8192]{2,1,0:T(8,128)(2,1)} %all-gather.3.cloned.1.call-done, bf16[256,16384]{1,0:T(8,128)(2,1)} %constant_dynamic-update-slice_fusion, s32[]{:T(128)S(6)} %select_n.48), kind=kOutput, calls=%fused_computation.21 | convolution fusion | flops 4295229440 | bytes 21495812 | tf_op jit(solution)/shard_map/sd,hd->sh/dot_general | solution.py:70
  140.7 0.3 copy.31
  141.0 3.8 %multiply_reduce_fusion.1 = (f32[2,512]{1,0:T(2,128)S(1)}, f32[2,512]{1,0:T(2,128)S(1)}, bf16[2,512,128]{2,1,0:T(8,128)(2,1)S(1)}) fusion(bf16[2,1024,128]{2,1,0:T(8,128)(2,1)S(1)} %bitcast.101, bf16[2,512,128]{2,1,0:T(8,128)(2,1)S(1)} %convolution_convert_fusion.1, bf16[1,1024,256]{2,1,0:T(8,128)(2,1)S(1)} %copy-done, s32[]{:T(128)S(6)} %select_n.45, ...), kind=kOutput, calls=%fused_computation.35 | convolution fusion | flops 273807360 | bytes 6041604 | tf_op jit(solution)/shard_map/hqk,kd->hqd/dot_general | solution.py:61
  144.8 0.2 copy.39
  145.0 12.7 %fusion = f32[256,8192]{1,0:T(8,128)} fusion(bf16[1024,256]{0,1:T(8,128)(2,1)S(1)} %bitcast.94, bf16[1,1024,8192]{2,1,0:T(8,128)(2,1)} %all-gather.3.cloned.1.call-done), kind=kOutput, calls=%fused_computation | convolution fusion | flops 4294967296 | bytes 25690112 | tf_op jit(solution)/shard_map/sh,sd->hd/dot_general | solution.py:73
  157.7 0.0 reduce-scatter.2.cloned.1.call-update
  157.8 3.4 %convolution_bitcast_fusion = f32[1024,128]{1,0:T(8,128)S(1)} fusion(bf16[2,1024,128]{2,1,0:T(8,128)(2,1)S(1)} %bitcast.102, f32[1024,2,512]{2,0,1:T(8,128)} %copy-done.3, f32[2,512]{1,0:T(2,128)S(1)} %log_add_fusion, pred[512,1024]{0,1:T(8,128)(4,1)S(1)} %get-tuple-element.94), kind=kOutput, calls=%fused_computation.22 | convolution fusion | flops 272629760 | bytes 5509120 | tf_op jit(solution)/shard_map/hqk,hqd->kd/dot_general | solution.py:106
  161.2 0.1 copy-done.2
  161.2 1.3 fusion.17
  162.5 0.1 collective-permute-start.8
  162.6 1.3 copy-done.4
  163.9 2.7 multiply_convert_fusion
  166.6 0.7 convolution_bitcast_fusion.2
  167.3 0.0 copy-start.18
  167.3 1.7 multiply_convert_fusion.1
  169.1 0.8 convolution_convert_fusion.2
  169.8 0.7 fusion.16
  170.6 0.8 convolution_convert_fusion
  171.3 0.1 collective-permute-start.7
  171.5 0.2 copy.38
  171.7 1.0 copy.40
  172.7 1.6 fusion.45
  174.3 0.7 fusion.44
  175.0 127.2 %reduce-scatter.2.cloned.1.call-done = f32[256,1024]{1,0:T(8,128)} async-done(((f32[256,8192]{1,0:T(8,128)}), f32[256,1024]{1,0:T(8,128)}) %reduce-scatter.2.cloned.1.call-update) | async-done | bytes 1048592 | tf_op jit(solution)/shard_map/reduce_scatter | solution.py:74
  (53 shorter events, 0.3 us)
Async XLA Ops:
  7.2 89.9 %copy-start = (bf16[1,1024,256]{2,1,0:T(8,128)(2,1)S(1)}, bf16[1,1024,256]{2,1,0:T(8,128)(2,1)}, u32[]{:S(2)}) copy-start(bf16[1,1024,256]{2,1,0:T(8,128)(2,1)} %param.24) | copy-start | bytes 1572868
  7.2 1.1 copy-start.5
  7.2 34.8 %copy-start.19 = (s32[1,4]{1,0:T(1,128)S(1)}, s32[1,4]{1,0:T(1,128)}, u32[]{:S(2)}) copy-start(s32[1,4]{1,0:T(1,128)} %param.27) | copy-start | bytes 52
  7.2 35.0 %copy-start.14 = (bf16[1,1024,256]{2,1,0:T(8,128)(2,1)S(1)}, bf16[1,1024,256]{2,1,0:T(8,128)(2,1)}, u32[]{:S(2)}) copy-start(bf16[1,1024,256]{2,1,0:T(8,128)(2,1)} %param.22) | copy-start | bytes 1572868
  7.2 121.9 %all-gather.3.cloned.1.call-start = ((), (), s32[]{:S(2)}) async-start(), calls=%async_computation.2 | async-start | bytes 20971520 | tf_op jit(solution)/shard_map/all_gather | solution.py:69
  7.9 294.3 %reduce-scatter.2.cloned.1.call-start = ((), (), s32[]{:S(2)}) async-start(), calls=%async_computation.1 | async-start | bytes 9437184 | tf_op jit(solution)/shard_map/reduce_scatter | solution.py:74
  8.3 18.0 %collective-permute-start = (bf16[256,1024]{1,0:T(8,128)(2,1)S(1)}, bf16[256,1024]{1,0:T(8,128)(2,1)S(1)}, u32[]{:S(2)}, u32[]{:S(2)}) collective-permute-start(bf16[256,1024]{1,0:T(8,128)(2,1)S(1)} %copy-done.5), channel_id=1, source_target_pairs={{0,4},{4,8},{8,12},{12,16},{16,20},{20,24},{24,28},{28,0},{1,5},{5... | collective-permute-start | bytes 1572872 | tf_op jit(solution)/shard_map/ppermute | solution.py:32
  26.2 15.8 %collective-permute-start.1 = (bf16[256,1024]{1,0:T(8,128)(2,1)S(1)}, bf16[256,1024]{1,0:T(8,128)(2,1)S(1)}, u32[]{:S(2)}, u32[]{:S(2)}) collective-permute-start(bf16[256,1024]{1,0:T(8,128)(2,1)S(1)} %collective-permute-done), channel_id=1, source_target_pairs={{0,4},{4,8},{8,12},{12,16},{16,20},{20,24},{24,28},{28,0},{1,5},{5... | collective-permute-start | bytes 1572872 | tf_op jit(solution)/shard_map/ppermute | solution.py:32
  42.0 15.0 %collective-permute-start.2 = (bf16[256,1024]{1,0:T(8,128)(2,1)S(1)}, bf16[256,1024]{1,0:T(8,128)(2,1)}, u32[]{:S(2)}, u32[]{:S(2)}) collective-permute-start(bf16[256,1024]{1,0:T(8,128)(2,1)S(1)} %collective-permute-done.1), channel_id=1, source_target_pairs={{0,4},{4,8},{8,12},{12,16},{16,20},{20,24},{24,28},{28,0},{1,5},{5... | collective-permute-start | bytes 1572872 | tf_op jit(solution)/shard_map/ppermute | solution.py:32
  43.4 30.1 %copy-start.10 = (bf16[1024,2,128]{2,0,1:T(8,128)(2,1)S(1)}, bf16[1024,2,128]{2,0,1:T(8,128)(2,1)}, u32[]{:S(2)}) copy-start(bf16[1024,2,128]{2,0,1:T(8,128)(2,1)} %copy.30) | copy-start | bytes 1572868
  43.4 30.1 %copy-start.17 = (bf16[1,1024,256]{2,1,0:T(8,128)(2,1)S(1)}, bf16[1,1024,256]{2,1,0:T(8,128)(2,1)}, u32[]{:S(2)}) copy-start(bf16[1,1024,256]{2,1,0:T(8,128)(2,1)} %param.23) | copy-start | bytes 1572868
  57.1 14.3 %collective-permute-start.3 = (bf16[256,1024]{1,0:T(8,128)(2,1)}, bf16[256,1024]{1,0:T(8,128)(2,1)S(1)}, u32[]{:S(2)}, u32[]{:S(2)}) collective-permute-start(bf16[256,1024]{1,0:T(8,128)(2,1)} %collective-permute-done.2), channel_id=1, source_target_pairs={{0,4},{4,8},{8,12},{12,16},{16,20},{20,24},{24,28},{28,0},{1,5},{5... | collective-permute-start | bytes 1572872 | tf_op jit(solution)/shard_map/ppermute | solution.py:32
  71.3 3.1 %copy-start.6 = (bf16[256,1024]{1,0:T(8,128)(2,1)}, bf16[256,1024]{1,0:T(8,128)(2,1)S(1)}, u32[]{:S(2)}) copy-start(bf16[256,1024]{1,0:T(8,128)(2,1)S(1)} %collective-permute-done.3) | copy-start | bytes 1572868
  71.3 13.2 %collective-permute-start.4 = (bf16[256,1024]{1,0:T(8,128)(2,1)S(1)}, bf16[256,1024]{1,0:T(8,128)(2,1)S(1)}, u32[]{:S(2)}, u32[]{:S(2)}) collective-permute-start(bf16[256,1024]{1,0:T(8,128)(2,1)S(1)} %collective-permute-done.3), channel_id=1, source_target_pairs={{0,4},{4,8},{8,12},{12,16},{16,20},{20,24},{24,28},{28,0},{1,5},{5... | collective-permute-start | bytes 1572872 | tf_op jit(solution)/shard_map/ppermute | solution.py:32
  73.5 13.0 %copy-start.1 = (f32[1024,2,512]{2,0,1:T(8,128)}, f32[1024,2,512]{2,0,1:T(8,128)S(1)}, u32[]{:S(2)}) copy-start(f32[1024,2,512]{2,0,1:T(8,128)S(1)} %get-tuple-element.99) | copy-start | bytes 12582916
  74.5 12.1 %copy-start.3 = (f32[1024,2,512]{2,0,1:T(8,128)}, f32[1024,2,512]{2,0,1:T(8,128)S(1)}, u32[]{:S(2)}) copy-start(f32[1024,2,512]{2,0,1:T(8,128)S(1)} %get-tuple-element.101) | copy-start | bytes 12582916
  84.6 2.0 copy-start.8
  84.6 12.5 %collective-permute-start.5 = (bf16[256,1024]{1,0:T(8,128)(2,1)S(1)}, bf16[256,1024]{1,0:T(8,128)(2,1)}, u32[]{:S(2)}, u32[]{:S(2)}) collective-permute-start(bf16[256,1024]{1,0:T(8,128)(2,1)S(1)} %collective-permute-done.4), channel_id=1, source_target_pairs={{0,4},{4,8},{8,12},{12,16},{16,20},{20,24},{24,28},{28,0},{1,5},{5... | collective-permute-start | bytes 1572872 | tf_op jit(solution)/shard_map/ppermute | solution.py:32
  97.0 12.2 %collective-permute-start.6 = (bf16[256,1024]{1,0:T(8,128)(2,1)}, bf16[256,1024]{1,0:T(8,128)(2,1)}, u32[]{:S(2)}, u32[]{:S(2)}) collective-permute-start(bf16[256,1024]{1,0:T(8,128)(2,1)} %collective-permute-done.5), channel_id=1, source_target_pairs={{0,4},{4,8},{8,12},{12,16},{16,20},{20,24},{24,28},{28,0},{1,5},{5... | collective-permute-start | bytes 1572872 | tf_op jit(solution)/shard_map/ppermute | solution.py:32
  97.1 16.0 %copy-start.9 = (bf16[256,1024]{1,0:T(8,128)(2,1)S(1)}, bf16[256,1024]{1,0:T(8,128)(2,1)}, u32[]{:S(2)}) copy-start(bf16[256,1024]{1,0:T(8,128)(2,1)} %copy-done.8) | copy-start | bytes 1572868
  97.1 16.8 %copy-start.7 = (bf16[256,1024]{1,0:T(8,128)(2,1)S(1)}, bf16[256,1024]{1,0:T(8,128)(2,1)}, u32[]{:S(2)}) copy-start(bf16[256,1024]{1,0:T(8,128)(2,1)} %copy-done.6) | copy-start | bytes 1572868
  141.0 20.2 %copy-start.15 = (bf16[1024,2,128]{2,0,1:T(8,128)(2,1)}, bf16[1024,2,128]{2,0,1:T(8,128)(2,1)S(1)}, u32[]{:S(2)}) copy-start(bf16[1024,2,128]{2,0,1:T(8,128)(2,1)S(1)} %copy.31) | copy-start | bytes 1572868
  157.8 3.5 %copy-start.2 = (f32[1024,2,512]{2,0,1:T(8,128)S(1)}, f32[1024,2,512]{2,0,1:T(8,128)}, u32[]{:S(2)}) copy-start(f32[1024,2,512]{2,0,1:T(8,128)} %copy-done.1) | copy-start | bytes 12582916
  161.2 2.6 copy-start.4
  162.5 4.1 %copy-start.12 = (f32[1024,128]{1,0:T(8,128)}, f32[1024,128]{1,0:T(8,128)S(1)}, u32[]{:S(2)}) copy-start(f32[1024,128]{1,0:T(8,128)S(1)} %fusion.17) | copy-start | bytes 1572868
  162.5 10.2 %collective-permute-start.8 = (f32[512,128]{1,0:T(8,128)S(1)}, f32[512,128]{1,0:T(8,128)}, u32[]{:S(2)}, u32[]{:S(2)}) collective-permute-start(f32[512,128]{1,0:T(8,128)S(1)} %constant_dynamic-slice_fusion), channel_id=1, source_target_pairs={{0,1},{1,0},{2,3},{3,2},{4,5},{5,4},{6,7},{7,6},{8,9},{9,8},{10,11... | collective-permute-start | bytes 786440 | tf_op jit(solution)/shard_map/ppermute | solution.py:12
  163.9 2.7 copy-start.11
  163.9 3.5 %copy-start.16 = (bf16[1024,2,128]{2,0,1:T(8,128)(2,1)S(1)}, bf16[1024,2,128]{2,0,1:T(8,128)(2,1)}, u32[]{:S(2)}) copy-start(bf16[1024,2,128]{2,0,1:T(8,128)(2,1)} %copy-done.15) | copy-start | bytes 1572868
  167.3 1.7 copy-start.18
  169.8 2.9 copy-start.13
  171.3 3.0 collective-permute-start.7
Sparse Core Ops, SparseCore 0:
  9.6 108.6 all-gather.2
  157.9 144.2 reduce-scatter.1
